TPU v7x, 32 devices: a whole 2x2x4 slice. The times are simulated.
32 devices in a mesh: pb: 4 (over z), row: 4 (over y, x), col: 2 (over core).
Axes of the slice: x: 2, y: 2, z: 4, core: 2. Of those that a mesh axis runs over, the one named last changes fastest.
Arguments:
- amplitudes: bfloat16 [4, 20, 4, 9216], P('pb'), may hold values from -6 to 6
- pairs: int32 [4, 4, 2], P('pb'), may hold values from 0 to 3
- stored_k: int32 [4], replicated, may hold values from 0 to 3, each once
- orbitals: bfloat16 [4, 192, 2048], P('pb', None, ('row', 'col')), may hold values from -1.078125 to 1.078125
- valence_energy: float32 [4, 96], replicated, may hold values from -1 to 0
- conduction_energy: float32 [4, 96], replicated, may hold values from 2.5 to 3.5
- screened: bfloat16 [4, 2048, 2048], P('pb', 'row', 'col'), may hold values from -0.125 to 0.125
Outputs:
- filtered: bfloat16 [4, 20, 4, 9216], P('pb')
Inputs may be any that keep to these rules, and one draw needn't show every extreme that they name: stored_k holds every k-point exactly once; row s of orbitals belongs to k-point stored_k[s]. `pairs`: each entry is a k-point.
All inputs are finite; a program needn't handle non-finite values.
Results may differ from a plain program's by a relative error of at most 0.024.
Values may be sent and summed in bfloat16 or wider, within the bound.
A program may use at most 64 MiB of HBM per device.

v0:
```python
import jax
import jax.numpy as jnp
from jax import lax
from jax.sharding import PartitionSpec as P

CENTER = 3.0
HALF = 2.5


def on_device(amplitudes, pairs, stored_k, orbitals, valence_energy, conduction_energy, screened):
    amplitude = amplitudes[0]
    pair_list = pairs[0]
    w_tile = screened[0]
    count_v = valence_energy.shape[1]
    count_c = conduction_energy.shape[1]
    vectors, pair_count, flat_size = amplitude.shape
    points = orbitals.shape[2]
    col_width = w_tile.shape[1]
    column = lax.axis_index("col")

    def pick(shard_piece):
        pick_low = (stored_k[None, :] == pair_list[:, 0:1]).astype(jnp.bfloat16)
        pick_high = (stored_k[None, :] == pair_list[:, 1:2]).astype(jnp.bfloat16)
        low_bands = jnp.einsum(
            "pl,lbr->pbr", pick_low, shard_piece[:, :count_v], preferred_element_type=jnp.float32
        )
        high_bands = jnp.einsum(
            "pl,lbr->pbr", pick_high, shard_piece[:, count_v:], preferred_element_type=jnp.float32
        )
        return (low_bands, high_bands)

    def fetch_each():
        found = pick(lax.all_gather(orbitals, "pb", axis=0, tiled=True))
        return (found[0].astype(jnp.bfloat16), found[1].astype(jnp.bfloat16))

    low_energy = jnp.take(valence_energy, pair_list[:, 0], axis=0)
    high_energy = jnp.take(conduction_energy, pair_list[:, 1], axis=0)
    gap_grid = (high_energy[:, None, :] - low_energy[:, :, None]).reshape(pair_count, flat_size)
    gap_rows = jnp.tile(gap_grid, (vectors, 1))

    def kernel_term(current, bands):
        valence, conduction_orbital = bands
        amplitude_lattice = current.reshape(vectors, pair_count, count_v, count_c)
        inner_total_sum = jnp.einsum(
            "iomx,oxj->iomj",
            amplitude_lattice,
            conduction_orbital,
            preferred_element_type=jnp.float32,
        )
        values = jnp.sum(valence.astype(jnp.float32)[None] * inner_total_sum, axis=2)
        values = values.astype(jnp.bfloat16).reshape(vectors * pair_count, points)
        everywhere = lax.all_gather(values, ("row", "col"), axis=1, tiled=True)
        needed = lax.dynamic_slice_in_dim(everywhere, column * col_width, col_width, 1)
        partial_value = lax.dot_general(
            needed, w_tile, (((1,), (1,)), ((), ())), preferred_element_type=jnp.float32
        )
        own_sums = (
            lax.psum_scatter(
                partial_value.astype(jnp.bfloat16), "col", scatter_dimension=1, tiled=True
            )
            .astype(jnp.float32)
            .reshape(vectors, pair_count, points)
        )
        weighted_product = (valence.astype(jnp.float32)[None] * own_sums[:, :, None, :]).astype(
            jnp.bfloat16
        )
        projected = jnp.einsum(
            "kyqz,yhz->kyqh",
            weighted_product,
            conduction_orbital,
            preferred_element_type=jnp.float32,
        )
        return projected.reshape(vectors * pair_count, flat_size)

    def advance(current_rows, summed, gap_part, previous_rows, factor):
        value = (gap_part * current_rows + summed - CENTER * current_rows) / HALF
        if previous_rows is None:
            return value.astype(jnp.bfloat16)
        return (factor * value - previous_rows).astype(jnp.bfloat16)

    def finish(partial_term, current, previous, factor):
        summed = lax.psum(partial_term.astype(jnp.bfloat16), ("row", "col")).astype(jnp.float32)
        previous_full = None
        if previous is not None:
            previous_full = previous.astype(jnp.float32)
        return advance(current.astype(jnp.float32), summed, gap_rows, previous_full, factor)

    initial = amplitude.reshape(vectors * pair_count, flat_size)
    first_bands = fetch_each()
    first_term = finish(kernel_term(initial, first_bands), initial, None, 1.0)
    second_bands = fetch_each()
    second_term = finish(kernel_term(first_term, second_bands), first_term, initial, 2.0)
    return second_term.reshape(1, vectors, pair_count, flat_size)


def solution(mesh):
    return jax.shard_map(
        on_device,
        mesh=mesh,
        in_specs=(
            P("pb", None, None, None),
            P("pb", None, None),
            P(),
            P("pb", None, ("row", "col")),
            P(),
            P(),
            P("pb", "row", "col"),
        ),
        out_specs=P("pb", None, None, None),
        check_vma=False,
    )
```

profile of v0, /device:TPU:0, one launch (start us, length us, event | category | flops | bytes accessed | tf_op | source)
XLA Modules:
  0.0 231.6 jit_solution(977043757335007725)
XLA Ops:
  6.5 0.8 slice_bitcast_fusion.1
  7.4 16.6 %all_gather.10 = bf16[4,192,256]{2,1,0:T(8,128)(2,1)S(1)} all-gather(bf16[1,192,256]{2,1,0:T(8,128)(2,1)} %param.12), channel_id=1, replica_groups=mesh['pb'=4,'row'=4,'col'=2] {'pb'}, dimensions={0}, use_global_device_ids=true | all-gather | bytes 491520 | tf_op jit(solution)/shard_map/all_gather | solution.py:33
  24.0 1.0 fusion.15
  25.0 0.1 copy.59
  25.1 2.6 %reshape_reshape_squeeze.3 = bf16[20,4,96,96]{3,2,1,0:T(8,128)(2,1)} reshape(bf16[1,20,4,9216]{3,2,1,0:T(4,128)(2,1)S(1)} %copy-done.1) | data formatting | bytes 2949120 | tf_op jit(solution)/shard_map/reshape;reshape;squeeze | solution.py:43
  27.7 0.3 fusion.16
  28.0 2.8 %fusion.1 = bf16[20,4,256]{2,0,1:T(8,128)(2,1)S(1)} fusion(f32[4,96,256]{2,1,0:T(8,128)S(1)} %copy.59, bf16[20,4,96,96]{3,2,1,0:T(8,128)(2,1)} %reshape_reshape_squeeze.3, bf16[4,96,256,1]{2,0,1,3:T(4,128)(2,1)S(1)} %fusion.16), kind=kOutput, calls=%fused_computation.5 | convolution fusion | flops 381399040 | bytes 2105344 | tf_op jit(solution)/shard_map/iomx,oxj->iomj/dot_general | solution.py:44
  30.8 0.0 copy-done.6
  30.9 10.1 %all_gather.11 = bf16[80,2048]{1,0:T(8,128)(2,1)S(1)} all-gather(bf16[80,256]{1,0:T(8,128)(2,1)S(1)} %convert_element_type.92), channel_id=1, replica_groups=mesh['pb'=4,'row'=4,'col'=2] {'row','col'}, dimensions={1}, use_global_device_ids=true | all-gather | bytes 368640 | tf_op jit(solution)/shard_map/all_gather | solution.py:52
  41.0 1.1 convolution_convert_fusion.3
  42.1 0.0 reduce-scatter.3.cloned.1.call-update
  42.1 0.0 all-reduce.3.cloned.1.call-start
  42.2 1.7 reshape.48
  43.9 6.7 %reduce-scatter.3.cloned.1.call-done = bf16[80,256]{1,0:T(8,128)(2,1)} async-done(((bf16[80,512]{1,0:T(8,128)(2,1)}), bf16[80,256]{1,0:T(8,128)(2,1)}) %reduce-scatter.3.cloned.1.call-update) | async-done | bytes 40976 | tf_op jit(solution)/shard_map/reduce_scatter | solution.py:58
  50.6 0.8 reshape.49
  51.4 0.0 copy-done.7
  51.4 2.9 %convert_bitcast_fusion.1 = bf16[20,4,96,96]{2,3,0,1:T(8,128)(2,1)} fusion(f32[20,4,256]{2,0,1:T(8,128)S(1)} %copy.63, f32[4,96,256]{2,1,0:T(8,128)S(1)} %copy.59, bf16[4,96,256,1]{2,0,1,3:T(4,128)(2,1)S(1)} %copy-done.7), kind=kOutput, calls=%fused_computation.25 | convolution fusion | flops 382156800 | bytes 2146304 | tf_op jit(solution)/shard_map/kyqz,yhz->kyqh/dot_general | solution.py:67
  54.3 3.2 %copy.65 = bf16[20,4,96,96]{3,2,1,0:T(8,128)(2,1)S(1)} copy(bf16[20,4,96,96]{2,3,0,1:T(8,128)(2,1)} %convert_bitcast_fusion.1) | data formatting | bytes 2949120 | tf_op jit(solution)/shard_map/convert_element_type | solution.py:82
  57.5 0.0 copy-start.2
  57.5 0.0 copy-start.3
  57.6 3.6 %convert_element_type.97 = bf16[80,9216]{1,0:T(8,128)(2,1)} reshape(bf16[20,4,96,96]{3,2,1,0:T(8,128)(2,1)S(1)} %copy.65) | data formatting | bytes 2949120 | tf_op jit(solution)/shard_map/convert_element_type | solution.py:82
  61.1 0.0 all-reduce.3.cloned.1.call-update
  61.1 0.0 reduce-scatter.5.cloned.1.call-start
  61.2 0.6 gather_fusion.1
  61.8 0.6 gather_fusion
  62.3 0.1 broadcast_select_fusion
  62.4 0.1 broadcast_select_fusion.1
  62.5 0.1 broadcast_subtract_fusion
  62.6 0.2 sub.32
  62.8 2.3 tile.8
  65.0 4.3 %tile.9 = f32[80,9216]{1,0:T(8,128)} reshape(f32[20,4,9216]{2,1,0:T(4,128)} %tile.8) | data formatting | bytes 5898240 | tf_op jit(solution)/shard_map/tile | solution.py:39
  69.3 51.5 %all-reduce.3.cloned.1.call-done = bf16[80,9216]{1,0:T(8,128)(2,1)} async-done(((bf16[80,9216]{1,0:T(8,128)(2,1)}), bf16[80,9216]{1,0:T(8,128)(2,1)}) %all-reduce.3.cloned.1.call-update) | async-done | bytes 1474576 | tf_op jit(solution)/shard_map/psum | solution.py:82
  120.8 3.8 %multiply_convert_fusion.4 = bf16[80,9216]{1,0:T(8,128)(2,1)S(1)} fusion(f32[80,9216]{1,0:T(8,128)} %reshape.48, bf16[80,9216]{1,0:T(8,128)(2,1)} %all-reduce.3.cloned.1.call-done, f32[80,9216]{1,0:T(8,128)} %tile.9), kind=kLoop, calls=%fused_computation.21 | loop fusion | flops 5160960 | bytes 8847360 | tf_op jit(solution)/shard_map/convert_element_type | solution.py:78
  124.6 2.9 %reshape.46 = bf16[20,4,96,96]{3,2,1,0:T(8,128)(2,1)} reshape(bf16[80,9216]{1,0:T(8,128)(2,1)S(1)} %multiply_convert_fusion.4) | data formatting | bytes 2949120 | tf_op jit(solution)/shard_map/reshape | solution.py:43
  127.6 2.7 %fusion = bf16[20,4,256]{2,0,1:T(8,128)(2,1)S(1)} fusion(f32[4,96,256]{2,1,0:T(8,128)S(1)} %copy.59, bf16[20,4,96,96]{3,2,1,0:T(8,128)(2,1)} %reshape.46, bf16[4,96,256,1]{2,0,1,3:T(4,128)(2,1)S(1)} %copy-done.8), kind=kOutput, calls=%fused_computation.3 | convolution fusion | flops 381399040 | bytes 2105344 | tf_op jit(solution)/shard_map/iomx,oxj->iomj/dot_general | solution.py:44
  130.4 9.5 %all_gather.12 = bf16[80,2048]{1,0:T(8,128)(2,1)S(1)} all-gather(bf16[80,256]{1,0:T(8,128)(2,1)S(1)} %convert_element_type.102), channel_id=1, replica_groups=mesh['pb'=4,'row'=4,'col'=2] {'row','col'}, dimensions={1}, use_global_device_ids=true | all-gather | bytes 368640 | tf_op jit(solution)/shard_map/all_gather | solution.py:52
  139.8 1.1 convolution_convert_fusion.2
  140.9 0.0 reduce-scatter.5.cloned.1.call-update
  140.9 0.2 all-reduce.5.cloned.1.call-start
  141.2 7.4 %reduce-scatter.5.cloned.1.call-done = bf16[80,256]{1,0:T(8,128)(2,1)} async-done(((bf16[80,512]{1,0:T(8,128)(2,1)}), bf16[80,256]{1,0:T(8,128)(2,1)}) %reduce-scatter.5.cloned.1.call-update) | async-done | bytes 40976 | tf_op jit(solution)/shard_map/reduce_scatter | solution.py:58
  148.6 0.8 reshape.50
  149.4 2.9 %convert_bitcast_fusion = bf16[20,4,96,96]{2,3,0,1:T(8,128)(2,1)} fusion(f32[20,4,256]{2,0,1:T(8,128)S(1)} %copy.69, f32[4,96,256]{2,1,0:T(8,128)S(1)} %copy.59, bf16[4,96,256,1]{2,0,1,3:T(4,128)(2,1)S(1)} %copy-done.8), kind=kOutput, calls=%fused_computation.24 | convolution fusion | flops 382156800 | bytes 2146304 | tf_op jit(solution)/shard_map/kyqz,yhz->kyqh/dot_general | solution.py:67
  152.3 3.2 %copy.71 = bf16[20,4,96,96]{3,2,1,0:T(8,128)(2,1)S(1)} copy(bf16[20,4,96,96]{2,3,0,1:T(8,128)(2,1)} %convert_bitcast_fusion) | data formatting | bytes 2949120 | tf_op jit(solution)/shard_map/convert_element_type | solution.py:82
  155.5 3.6 %convert_element_type.107 = bf16[80,9216]{1,0:T(8,128)(2,1)} reshape(bf16[20,4,96,96]{3,2,1,0:T(8,128)(2,1)S(1)} %copy.71) | data formatting | bytes 2949120 | tf_op jit(solution)/shard_map/convert_element_type | solution.py:82
  159.1 0.0 all-reduce.5.cloned.1.call-update
  159.1 59.7 %all-reduce.5.cloned.1.call-done = bf16[80,9216]{1,0:T(8,128)(2,1)} async-done(((bf16[80,9216]{1,0:T(8,128)(2,1)}), bf16[80,9216]{1,0:T(8,128)(2,1)}) %all-reduce.5.cloned.1.call-update) | async-done | bytes 1474576 | tf_op jit(solution)/shard_map/psum | solution.py:82
  218.8 4.8 %fusion.12 = bf16[80,9216]{1,0:T(8,128)(2,1)S(1)} fusion(f32[80,9216]{1,0:T(8,128)} %reshape.48, f32[80,9216]{1,0:T(8,128)} %tile.9, bf16[80,9216]{1,0:T(8,128)(2,1)} %all-reduce.5.cloned.1.call-done, bf16[80,9216]{1,0:T(8,128)(2,1)} %all-reduce.3.cloned.1.call-done), kind=kLoop, calls=%fused_computation.20 | loop fusion | flops 11796480 | bytes 10321920 | tf_op jit(solution)/shard_map/convert_element_type | solution.py:79
  223.6 1.4 reshape.47
  (24 shorter events, 0.2 us)
Async XLA Ops:
  6.5 34.5 %copy-start = (bf16[1,512,1024]{2,1,0:T(8,128)(2,1)S(1)}, bf16[1,512,1024]{2,1,0:T(8,128)(2,1)}, u32[]{:S(2)}) copy-start(bf16[1,512,1024]{2,1,0:T(8,128)(2,1)} %param.15) | copy-start | bytes 3145732
  6.5 18.5 %copy-start.1 = (bf16[1,20,4,9216]{3,2,1,0:T(4,128)(2,1)S(1)}, bf16[1,20,4,9216]{3,2,1,0:T(4,128)(2,1)}, u32[]{:S(2)}) copy-start(bf16[1,20,4,9216]{3,2,1,0:T(4,128)(2,1)} %param.9) | copy-start | bytes 4423684
  6.5 44.1 %reduce-scatter.3.cloned.1.call-start = ((), (), s32[]{:S(2)}) async-start(), calls=%async_computation.2 | async-start | bytes 122880 | tf_op jit(solution)/shard_map/reduce_scatter | solution.py:58
  7.4 20.3 %copy-start.5 = (s32[4]{0:T(128)S(1)}, s32[4]{0:T(128)}, u32[]{:S(2)}) copy-start(s32[4]{0:T(128)} %param.11) | copy-start | bytes 52
  28.0 2.8 %copy-start.6 = (bf16[4,96,256,1]{2,0,1,3:T(4,128)(2,1)}, bf16[4,96,256,1]{2,0,1,3:T(4,128)(2,1)S(1)}, u32[]{:S(2)}) copy-start(bf16[4,96,256,1]{2,0,1,3:T(4,128)(2,1)S(1)} %fusion.16) | copy-start | bytes 589828
  41.0 2.9 %copy-start.4 = (s32[1,4,2]{1,2,0:T(2,128)S(1)}, s32[1,4,2]{1,2,0:T(2,128)}, u32[]{:S(2)}) copy-start(s32[1,4,2]{1,2,0:T(2,128)} %param.10) | copy-start | bytes 100
  42.1 9.3 %copy-start.7 = (bf16[4,96,256,1]{2,0,1,3:T(4,128)(2,1)S(1)}, bf16[4,96,256,1]{2,0,1,3:T(4,128)(2,1)}, u32[]{:S(2)}) copy-start(bf16[4,96,256,1]{2,0,1,3:T(4,128)(2,1)} %copy-done.6) | copy-start | bytes 589828
  42.1 78.7 %all-reduce.3.cloned.1.call-start = ((), (), s32[]{:S(2)}) async-start(), calls=%async_computation.3 | async-start | bytes 2949120 | tf_op jit(solution)/shard_map/psum | solution.py:82
  57.5 3.7 %copy-start.2 = (f32[4,96]{1,0:T(4,128)S(1)}, f32[4,96]{1,0:T(4,128)}, u32[]{:S(2)}) copy-start(f32[4,96]{1,0:T(4,128)} %param.13) | copy-start | bytes 4612
  57.5 4.2 %copy-start.3 = (f32[4,96]{1,0:T(4,128)S(1)}, f32[4,96]{1,0:T(4,128)}, u32[]{:S(2)}) copy-start(f32[4,96]{1,0:T(4,128)} %param.14) | copy-start | bytes 4612
  61.1 87.5 %reduce-scatter.5.cloned.1.call-start = ((), (), s32[]{:S(2)}) async-start(), calls=%async_computation.4 | async-start | bytes 122880 | tf_op jit(solution)/shard_map/reduce_scatter | solution.py:58
  124.6 2.9 %copy-start.8 = (bf16[4,96,256,1]{2,0,1,3:T(4,128)(2,1)S(1)}, bf16[4,96,256,1]{2,0,1,3:T(4,128)(2,1)}, u32[]{:S(2)}) copy-start(bf16[4,96,256,1]{2,0,1,3:T(4,128)(2,1)} %copy-done.6) | copy-start | bytes 589828
  140.9 77.9 %all-reduce.5.cloned.1.call-start = ((), (), s32[]{:S(2)}) async-start(), calls=%async_computation.5 | async-start | bytes 2949120 | tf_op jit(solution)/shard_map/psum | solution.py:82
Sparse Core Ops, SparseCore 0:
  42.2 8.3 reduce-scatter.2
  61.3 59.5 all-reduce.2
  141.1 7.5 reduce-scatter.4
  159.2 59.5 all-reduce.4
where the time goes:
time: 232 us
  waiting for transfers between devices  125 us (54%)
  blocking collectives  36.2 us (16%)
  local copies, waits for them, and re-layouts  32.7 us (14%)
  matrix products  14.8 us (6%)
  between operations  13.3 us (6%)
  other arithmetic  8.91 us (4%)
    psum x2, waiting for transfers between devices, finish(): lax.psum(partial_term.astype(jnp.bfloat16), ('row', 'col'))  111 us
    all_gather x2, blocking collectives, kernel_term(): everywhere = lax.all_gather(values, ('row', 'col'), axis=1, tiled=True)  19.6 us
    all_gather x1, blocking collectives, fetch_each(): found = pick(lax.all_gather(orbitals, 'pb', axis=0, tiled=True))  16.6 us
    reduce_scatter x2, waiting for transfers between devices, kernel_term(): lax.psum_scatter(partial_value.astype(jnp.bfloat16), 'col', scatter_dimen...  14.1 us
    convert_element_type x4, local copies, waits for them, and re-layouts, finish(): partial_term.astype(jnp.bfloat16)  13.5 us
    another operation x2, local copies, waits for them, and re-layouts, on_device(): gap_rows = jnp.tile(gap_grid, (vectors, 1))  6.56 us
    dot_general x2, matrix products, kernel_term(): jnp.einsum('kyqz,yhz->kyqh', weighted_product, conduction_orbital, prefer...  5.75 us
    dot_general x2, matrix products, kernel_term(): jnp.einsum('iomx,oxj->iomj', amplitude_lattice, conduction_orbital, prefe...  5.54 us
  transfers between devices with their start and end apart: 4, of which 4 were waited for; matrix products, arithmetic and copies ran while one was open for 4% of the time, Pallas kernels for 0%

commit v1 on v0

v1 whole, which is shorter than its diff:
```python
import functools
import math

import jax
import jax.numpy as jnp
from jax import lax
from jax.experimental import pallas as pl
from jax.experimental.pallas import tpu as pltpu
from jax.sharding import PartitionSpec as P

CENTER = 3.0
HALF = 2.5
LANES = 128
MESH = pl.DeviceIdType.MESH


def dot(a, b):
    return jnp.dot(a, b, preferred_element_type=jnp.float32)


def dot_t(a, b):
    return lax.dot_general(a, b, (((1,), (1,)), ((), ())), preferred_element_type=jnp.float32)


def windows(count_c):
    group = LANES // math.gcd(count_c, LANES)
    width = group * count_c
    length = min(width, -(-count_c // LANES) * LANES + LANES)
    starts = [min(j * count_c // LANES * LANES, width - length) for j in range(group)]
    offsets = [j * count_c - starts[j] for j in range(group)]
    return group, width, length, starts, offsets


def kernel(
    sizes, pairs, stored, amp, orb, ev, ec, w, out,
    zbuf, sel, obuf, vtmp, vj, pad, mfull, mrecv, nsend, nrecv, nfull, gbuf, gap, t1,
    z_s, z_r, z_l, o_s, o_r, f_s, f_r, m_s, m_r, n_s, n_r, g_s, g_r, h_s, h_r,
):
    n_pb, n_row, n_col, count_v, count_c, vecs, points, chunks = sizes
    group, width, length, starts, offsets = windows(count_c)
    inner = count_v // group
    top = max(offsets)
    blocks = n_row * n_col
    rows_pad = mfull.shape[1]
    total = blocks * points
    half_blocks = blocks // n_col
    z, row, col = lax.axis_index("pb"), lax.axis_index("row"), lax.axis_index("col")
    me = row * n_col + col

    def peer(step):
        dr, dc = divmod(step, n_col)
        return lax.rem(row + dr, n_row), lax.rem(col + dc, n_col)

    def source(step):
        dr, dc = divmod(step, n_col)
        return lax.rem(row + n_row - dr, n_row), lax.rem(col + n_col - dc, n_col)

    def to(r, c):
        return {"row": r, "col": c}

    def remote(src, dst, send, recv, device):
        return pltpu.make_async_remote_copy(
            src_ref=src, dst_ref=dst, send_sem=send, recv_sem=recv, device_id=device, device_id_type=MESH
        )

    barrier = pltpu.get_barrier_semaphore()
    for d in range(1, n_pb):
        pl.semaphore_signal(barrier, inc=1, device_id={"pb": lax.rem(z + d, n_pb)}, device_id_type=MESH)
    for step in range(1, blocks):
        pl.semaphore_signal(barrier, inc=1, device_id=to(*peer(step)), device_id_type=MESH)
    pl.semaphore_wait(barrier, n_pb - 1 + blocks - 1)

    z_copies = []
    for d in range(1, n_pb):
        copy = remote(orb, zbuf.at[z], z_s.at[d - 1], z_r.at[d - 1], {"pb": lax.rem(z + d, n_pb)})
        copy.start()
        z_copies.append(copy)
    local = pltpu.make_async_copy(orb, zbuf.at[z], z_l)
    local.start()
    pad[...] = jnp.zeros_like(pad)
    gap[...] = ec[pairs[row, 1]] - ev[pairs[row, 0]]
    local.wait()
    for copy in z_copies:
        copy.wait()

    def find(k):
        return lax.fori_loop(0, n_pb, lambda i, s: jnp.where(stored[i] == k, i, s), jnp.int32(0))

    def pick(p):
        low, high = find(pairs[p, 0]), find(pairs[p, 1])
        return zbuf[low, :count_v, :], zbuf[high, count_v:, :]

    o_copies, f_copies = [], []
    for d in range(1, n_row):
        p = lax.rem(row + d, n_row)
        low, high = pick(p)
        sel[d - 1, :count_v] = low
        sel[d - 1, count_v:] = high
        copy = remote(sel.at[d - 1], obuf.at[me], o_s.at[d - 1], o_r.at[d - 1], to(p, col))
        copy.start()
        o_copies.append(copy)
    low, high = pick(row)
    obuf[me, :count_v] = low
    obuf[me, count_v:] = high

    def forward(d, slot):
        for e in range(1, n_col):
            copy = remote(
                obuf.at[slot], obuf.at[slot], f_s.at[e - 1, d], f_r.at[e - 1, d], to(row, lax.rem(col + e, n_col))
            )
            copy.start()
            f_copies.append((e, d, copy))

    def span(slot):
        return pl.ds(pl.multiple_of(slot * points, points), points)

    def prepare(slot):
        for t in range(points // LANES):
            vtmp[t] = obuf[slot, :count_v, t * LANES : (t + 1) * LANES].astype(jnp.float32)
            at = pl.ds(pl.multiple_of(slot * points + t * LANES, LANES), LANES)
            for j in range(group):
                vj[j, :, at] = vtmp[t, pl.ds(j, inner, stride=group), :]
        pad[top : top + count_c, span(slot)] = obuf[slot, count_v:, :]

    def expand(source_ref, slot):
        acc = None
        for j in range(group):
            value = dot(
                source_ref[:, starts[j] : starts[j] + length],
                pad[top - offsets[j] : top - offsets[j] + length, span(slot)],
            ).reshape(vecs, inner, points)
            term = value * vj[j, :, span(slot)][None]
            acc = term if acc is None else acc + term
        m = jnp.sum(acc, axis=1)
        m = jnp.concatenate([m, jnp.zeros((rows_pad - vecs, points), jnp.float32)], axis=0)
        mfull[slot] = m.astype(jnp.bfloat16)

    forward(0, me)
    prepare(me)
    expand(amp, me)
    for d in range(1, n_row):
        o_copies[d - 1].wait_recv()
        slot = lax.rem(row + n_row - d, n_row) * n_col + col
        forward(d, slot)
        prepare(slot)
        expand(amp, slot)
    for e, d, copy in f_copies:
        copy.wait_recv()
        slot = lax.rem(row + n_row - d, n_row) * n_col + lax.rem(col + n_col - e, n_col)
        prepare(slot)
        expand(amp, slot)
    for copy in o_copies:
        copy.wait_send()
    for _, _, copy in f_copies:
        copy.wait_send()

    def screen():
        copies = []
        for step in range(1, blocks):
            r, c = peer(step)
            copy = remote(
                mfull.at[pl.ds(c * half_blocks, half_blocks)], mrecv.at[me], m_s.at[step - 1], m_r.at[step - 1], to(r, c)
            )
            copy.start()
            copies.append(copy)
        mrecv[me] = mfull[pl.ds(col * half_blocks, half_blocks)]
        for copy in copies:
            copy.wait()
        partial = None
        for i in range(half_blocks):
            term = dot_t(
                mrecv[:, i].reshape(blocks * rows_pad, points), w[:, i * points : (i + 1) * points]
            )
            partial = term if partial is None else partial + term
        nsend[...] = partial.astype(jnp.bfloat16).reshape(nsend.shape)
        copies = []
        for step in range(1, blocks):
            r, c = peer(step)
            copy = remote(
                nsend.at[r * n_col + c], nrecv.at[me], n_s.at[step - 1], n_r.at[step - 1], to(r, c)
            )
            copy.start()
            copies.append(copy)
        nrecv[me] = nsend[me]
        for copy in copies:
            copy.wait()
        span_row = n_col * points
        for r in range(n_row):
            value = nrecv[r * n_col].astype(jnp.float32)
            for c in range(1, n_col):
                value = value + nrecv[r * n_col + c].astype(jnp.float32)
            nfull[:, r * span_row : (r + 1) * span_row] = value

    def project(first, count):
        rows = count * inner
        parts = [None] * (width // LANES)
        for j in range(group):
            for g in range(blocks):
                at = slice(g * points, (g + 1) * points)
                value = vj[j, :, at][None] * nfull[first : first + count, at][:, None, :]
                gbuf[:rows, at] = value.reshape(rows, points).astype(jnp.bfloat16)
            result = dot_t(gbuf[:rows], pad[top - offsets[j] : top - offsets[j] + length, :])
            for i in range(length // LANES):
                tile = starts[j] // LANES + i
                piece = result[:, i * LANES : (i + 1) * LANES]
                parts[tile] = piece if parts[tile] is None else parts[tile] + piece
        return jnp.concatenate(parts, axis=1)

    def apply(current, first, count):
        rows = slice(first * inner, (first + count) * inner)
        value = current[rows, :].astype(jnp.float32)
        scaled = (value.reshape(count, inner, width) * (gap[...] - CENTER)[None]).reshape(count * inner, width)
        return (scaled + project(first, count)) * (1.0 / HALF)

    screen()
    t1[...] = apply(amp, 0, vecs).astype(jnp.bfloat16)

    @pl.loop(0, blocks)
    def _(slot):
        expand(t1, slot)

    screen()
    pending = []
    first = 0
    for i, count in enumerate(chunks):
        rows = slice(first * inner, (first + count) * inner)
        size = count * inner
        value = 2.0 * apply(t1, first, count) - amp[rows, :].astype(jnp.float32)
        out[me, rows, :] = value.astype(jnp.bfloat16)
        copies = []
        for d in range(1, n_row):
            copy = remote(
                out.at[me, pl.ds(first * inner, size)], out.at[me, pl.ds(first * inner, size)],
                g_s.at[i, d - 1], g_r.at[i, d - 1], to(lax.rem(row + d, n_row), col),
            )
            copy.start()
            copies.append(copy)
        pending.append((first * inner, size, copies))
        first += count
    handed = []
    for i, (start, size, copies) in enumerate(pending):
        for d in range(n_row):
            if d > 0:
                copies[d - 1].wait_recv()
            slot = lax.rem(row + n_row - d, n_row) * n_col + col
            for e in range(1, n_col):
                copy = remote(
                    out.at[slot, pl.ds(start, size)], out.at[slot, pl.ds(start, size)],
                    h_s.at[i, e - 1, d], h_r.at[i, e - 1, d], to(row, lax.rem(col + e, n_col)),
                )
                copy.start()
                handed.append(copy)
    for copy in handed:
        copy.wait()
    for _, _, copies in pending:
        for copy in copies:
            copy.wait_send()


def on_device(sizes, amplitudes, pairs, stored_k, orbitals, valence_energy, conduction_energy, screened):
    n_pb, n_row, n_col = sizes
    _, vectors, pair_count, flat = amplitudes.shape
    count_v, count_c = valence_energy.shape[1], conduction_energy.shape[1]
    points = orbitals.shape[2]
    bands = orbitals.shape[1]
    blocks = n_row * n_col
    assert pair_count == n_row and vectors % n_col == 0 and count_v + count_c == bands
    vecs = vectors // n_col
    group, width, length, starts, offsets = windows(count_c)
    inner = count_v // group
    top = max(offsets)
    rows = vecs * inner
    rows_pad = -(-vecs // 16) * 16
    step = max(1, 16 // math.gcd(inner, 16))
    chunks, left = [], vecs
    while left > 0:
        chunks.append(min(left, 2 * step))
        left -= chunks[-1]
    row, col = lax.axis_index("row"), lax.axis_index("col")
    own = lax.dynamic_slice(amplitudes[0], (col * vecs, row, 0), (vecs, 1, flat)).reshape(rows, width)
    ev = jnp.repeat(valence_energy.reshape(-1, inner, group), count_c, axis=2)
    ec = jnp.tile(conduction_energy, (1, group))[:, None, :]
    dma = pltpu.SemaphoreType.DMA
    bf16, f32 = jnp.bfloat16, jnp.float32
    kc = len(chunks)
    smem, vmem = pl.BlockSpec(memory_space=pltpu.SMEM), pl.BlockSpec(memory_space=pltpu.VMEM)
    gathered = pl.pallas_call(
        functools.partial(kernel, (n_pb, n_row, n_col, count_v, count_c, vecs, points, chunks)),
        out_shape=jax.ShapeDtypeStruct((blocks, rows, width), bf16),
        in_specs=[smem, smem, vmem, vmem, vmem, vmem, vmem],
        out_specs=vmem,
        scratch_shapes=[
            pltpu.VMEM((n_pb, bands, points), bf16),
            pltpu.VMEM((n_row, bands, points), bf16),
            pltpu.VMEM((blocks, bands, points), bf16),
            pltpu.VMEM((points // LANES, count_v, LANES), f32),
            pltpu.VMEM((group, inner, blocks * points), f32),
            pltpu.VMEM((top + length, blocks * points), bf16),
            pltpu.VMEM((blocks, rows_pad, points), bf16),
            pltpu.VMEM((blocks, blocks // n_col, rows_pad, points), bf16),
            pltpu.VMEM((blocks, rows_pad, n_col * points), bf16),
            pltpu.VMEM((blocks, rows_pad, n_col * points), bf16),
            pltpu.VMEM((rows_pad, blocks * points), f32),
            pltpu.VMEM((rows, blocks * points), bf16),
            pltpu.VMEM((inner, width), f32),
            pltpu.VMEM((rows, width), bf16),
            dma((max(1, n_pb - 1),)), dma((max(1, n_pb - 1),)), dma,
            dma((n_row,)), dma((n_row,)),
            dma((n_col, n_row)), dma((n_col, n_row)),
            dma((blocks,)), dma((blocks,)),
            dma((blocks,)), dma((blocks,)),
            dma((kc, n_row)), dma((kc, n_row)),
            dma((kc, n_col, n_row)), dma((kc, n_col, n_row)),
        ],
        compiler_params=pltpu.CompilerParams(
            collective_id=0, has_side_effects=True, vmem_limit_bytes=48 * 1024 * 1024
        ),
    )(pairs[0], stored_k, own, orbitals[0], ev, ec, screened[0])
    spread = gathered.reshape(pair_count, vectors, flat)
    return jnp.transpose(spread, (1, 0, 2))[None]


def solution(mesh):
    sizes = (mesh.shape["pb"], mesh.shape["row"], mesh.shape["col"])
    return jax.shard_map(
        functools.partial(on_device, sizes),
        mesh=mesh,
        in_specs=(
            P("pb", None, None, None),
            P("pb", None, None),
            P(),
            P("pb", None, ("row", "col")),
            P(),
            P(),
            P("pb", "row", "col"),
        ),
        out_specs=P("pb", None, None, None),
        check_vma=False,
    )
```

time: 232 us -> 68.1 us (0.29)
  waiting for transfers between devices: 125 us -> 0 us
  Pallas kernels: 0 us -> 56.8 us
  blocking collectives: 36.2 us -> 0 us
  local copies, waits for them, and re-layouts: 32.7 us -> 10.8 us
  matrix products: 14.8 us -> 0 us
  between operations: 13.3 us -> 0.08 us
  other arithmetic: 8.91 us -> 0 us
    psum x2 -> x0, waiting for transfers between devices: 111 us -> none  [finish(): lax.psum(partial_term.astype(jnp.bfloat16), ('row', 'col'))]
    pallas_call x0 -> x1, Pallas kernels: none -> 56.8 us  [on_device(): pl.pallas_call(functools.partial(kernel, (n_pb, n_row, n_col, count_v, co...]
    all_gather x3 -> x0, blocking collectives: 36.2 us -> none  [the longest x2 19.6 us: kernel_term(): everywhere = lax.all_gather(values, ('row', 'col'), axis=1, tiled=True)]
    convert_element_type x8 -> x0, local copies, waits for them, and re-layouts: 15.3 us -> none  [the longest x4 13.5 us: finish(): partial_term.astype(jnp.bfloat16)]
    dot_general x8 -> x0, matrix products: 14.8 us -> none  [the longest x2 5.75 us: kernel_term(): jnp.einsum('kyqz,yhz->kyqh', weighted_product, conduction_orbital, prefer...]
    reduce_scatter x2 -> x0, waiting for transfers between devices: 14.1 us -> none  [kernel_term(): lax.psum_scatter(partial_value.astype(jnp.bfloat16), 'col', scatter_dimen...]
    convert_element_type x2 -> x0, other arithmetic: 8.64 us -> none  [the longest x1 4.83 us: advance(): return (factor * value - previous_rows).astype(jnp.bfloat16)]
    another operation x3 -> x2, local copies, waits for them, and re-layouts: 9.13 us -> 0.77 us  [on_device(): ec = jnp.tile(conduction_energy, (1, group))[:, None, :]]
  transfers between devices with their start and end apart: 4 -> 0, of which waited for: 4 -> 0; matrix products, arithmetic and copies ran while one was open for 4% -> 0% of each run, Pallas kernels for 0% -> 0%
where the time goes in v1:
time: 68.1 us; the launch traced here: 67.7 us
  Pallas kernels  56.8 us (83%)
  local copies, waits for them, and re-layouts  10.8 us (16%)
    pallas_call x1, Pallas kernels, on_device(): pl.pallas_call(functools.partial(kernel, (n_pb, n_row, n_col, count_v, co...  56.8 us
    broadcast_in_dim x1, local copies, waits for them, and re-layouts, on_device(): return jnp.transpose(spread, (1, 0, 2))[None]  3.72 us
    reshape x1, local copies, waits for them, and re-layouts, on_device(): spread = gathered.reshape(pair_count, vectors, flat)  1.85 us

profile of v1, /device:TPU:0, one launch (start us, length us, event | category | flops | bytes accessed | tf_op | source)
XLA Modules:
  0.0 67.7 jit_solution(17574085941856139736)
XLA Ops:
  0.0 0.0 copy-start
  0.0 0.0 copy-start.2
  0.0 0.0 copy-start.3
  0.0 0.9 %copy.10.pairs = s32[4,2]{1,0:T(4,128)S(1)} copy(s32[4,2]{0,1:T(2,128)} %bitcast.9) | data formatting | bytes 64 | tf_op jit(solution)/shard_map/squeeze | solution.py:318
  0.9 0.7 %tile.8 = f32[4,4,96]{2,1,0:T(4,128)S(1)} broadcast(f32[4,96]{1,0:T(4,128)} %param.12), dimensions={0,2} | broadcast | bytes 7680 | tf_op jit(solution)/shard_map/tile | solution.py:282
  1.6 0.1 tile.9.ec
  1.7 0.8 %reshape.21 = f32[4,24,4]{2,1,0:T(8,128)S(1)} reshape(f32[4,96]{1,0:T(4,128)} %param.11) | data formatting | bytes 3072 | tf_op jit(solution)/shard_map/reshape | solution.py:281
  2.4 0.2 broadcast_in_dim.6
  2.6 0.1 reshape.22.ev
  2.8 0.0 copy-done
  2.8 1.1 %dynamic-slice_reduce_fusion = bf16[10,9216]{1,0:T(8,128)(2,1)S(1)} fusion(bf16[1,20,4,9216]{3,2,1,0:T(4,128)(2,1)S(1)} %copy-done, s32[]{:T(128)S(6)} %select_n.6, s32[]{:T(128)S(6)} %select_n.7), kind=kLoop, calls=%fused_computation | loop fusion | bytes 368648 | tf_op jit(solution)/shard_map/dynamic_slice | solution.py:280
  3.9 0.1 reshape.20.amp
  4.0 0.0 copy-done.2
  4.0 0.0 copy-done.3
  4.1 0.0 copy-start.1
  4.1 1.2 %copy-done.1 = bf16[1,512,1024]{2,1,0:T(8,128)(2,1)S(1)} copy-done((bf16[1,512,1024]{2,1,0:T(8,128)(2,1)S(1)}, bf16[1,512,1024]{2,1,0:T(8,128)(2,1)}, u32[]{:S(2)}) %copy-start.1) | copy-done | bytes 1048600
  5.3 56.8 %shard_map.73 = bf16[8,240,384]{2,1,0:T(8,128)(2,1)S(1)} custom-call(s32[4,2]{1,0:T(4,128)S(1)} %copy.10.pairs, s32[4]{0:T(128)S(1)} %copy-done.3, bf16[240,384]{1,0:T(8,128)(2,1)S(1)} %reshape.20.amp, bf16[192,256]{1,0:T(8,128)(2,1)S(1)} %bitcast.7, f32[4,24,384]{2,1,0:T(8,128)S(1)} %reshape.22.ev, f32[4,1,384]{2,1,0:T(1,128)S(1)} %tile.9.ec, ...), custom_call_target="tpu_custom_call" | custom-call | tf_op jit(solution)/shard_map/pallas_call | solution.py:287
  62.1 1.9 %reshape.23 = bf16[4,20,9216]{2,1,0:T(8,128)(2,1)} reshape(bf16[8,240,384]{2,1,0:T(8,128)(2,1)S(1)} %shard_map.73) | data formatting | bytes 2949120 | tf_op jit(solution)/shard_map/reshape | solution.py:319
  64.0 3.7 %copy.11 = bf16[1,20,4,9216]{3,2,1,0:T(4,128)(2,1)} copy(bf16[1,20,4,9216]{3,1,2,0:T(8,128)(2,1)} %bitcast.8) | data formatting | bytes 2949120 | tf_op jit(solution)/shard_map/broadcast_in_dim | solution.py:320
Async XLA Ops:
  0.0 2.8 %copy-start = (bf16[1,20,4,9216]{3,2,1,0:T(4,128)(2,1)S(1)}, bf16[1,20,4,9216]{3,2,1,0:T(4,128)(2,1)}, u32[]{:S(2)}) copy-start(bf16[1,20,4,9216]{3,2,1,0:T(4,128)(2,1)} %param.7) | copy-start | bytes 4423684
  0.0 4.0 %copy-start.2 = (bf16[1,192,256]{2,1,0:T(8,128)(2,1)S(1)}, bf16[1,192,256]{2,1,0:T(8,128)(2,1)}, u32[]{:S(2)}) copy-start(bf16[1,192,256]{2,1,0:T(8,128)(2,1)} %param.10) | copy-start | bytes 294916
  0.0 4.0 %copy-start.3 = (s32[4]{0:T(128)S(1)}, s32[4]{0:T(128)}, u32[]{:S(2)}) copy-start(s32[4]{0:T(128)} %stored.1) | copy-start | bytes 52
  4.1 1.2 %copy-start.1 = (bf16[1,512,1024]{2,1,0:T(8,128)(2,1)S(1)}, bf16[1,512,1024]{2,1,0:T(8,128)(2,1)}, u32[]{:S(2)}) copy-start(bf16[1,512,1024]{2,1,0:T(8,128)(2,1)} %param.13) | copy-start | bytes 3145732
